TPU v7x, 32 devices: a whole 2x2x4 slice. The times are simulated.
32 devices in a mesh: section: 4 (over x, core), blk: 4 (over z), tp: 2 (over y).
Axes of the slice: x: 2, y: 2, z: 4, core: 2. Of those that a mesh axis runs over, the one named last changes fastest.
Arguments:
- query: bfloat16 [2048, 8192], P(('section', 'blk'), 'tp'), may hold values from -6 to 6
- text_frame: int32 [2048], P(('section', 'blk')), may hold values from 0 to 63
- image_feats: bfloat16 [1024, 8192], P('blk', ('section', 'tp')), may hold values from -6 to 6
- image_frame: int32 [1024], P('blk'), may hold values from 0 to 63, never falling along the last dimension, each value on 1 to 32 neighbouring positions
- kv_weight: bfloat16 [4, 8192, 2, 1024], P('section', None, None, 'tp'), may hold values from -0.0625 to 0.0625
- query_gain: float32 [4, 128], P('section'), may hold values from 0.1 to 1.9
- key_gain: float32 [4, 128], P('section'), may hold values from 0.1 to 1.9
Outputs:
- attended: bfloat16 [2048, 8192], P(('section', 'blk'), 'tp')
Inputs may be any that keep to these rules, and one draw needn't show every extreme that they name: `image_frame`: image frame ids never fall along the image tokens; every frame has at least one token.
All inputs are finite; a program needn't handle non-finite values.
Results may differ from a plain program's by a relative error of at most 0.007.
Values may be sent and summed in bfloat16 or wider, within the bound.
A program may use at most 128 MiB of HBM per device.

v0:
```python
import jax
import jax.numpy as jnp
from jax import lax
from jax.sharding import PartitionSpec as P


def normalize(x):
    return x * lax.rsqrt(jnp.mean(x * x, axis=-1, keepdims=True) + 1e-05)


def per_device(query, text_frame, image_feats, image_frame, kv_weight, query_gain, key_gain):
    head_size = query_gain.shape[1]
    feat_width = kv_weight.shape[1]
    kv_cols = kv_weight.shape[3]
    heads_kv = kv_cols // head_size
    text_rows = query.shape[0]
    groups = query.shape[1] // kv_cols
    block_rows = image_feats.shape[0]
    weight_flat = kv_weight[0].reshape(feat_width, 2 * kv_cols)
    wide = lax.all_gather(image_feats, ("section", "tp"), axis=1, tiled=True)
    proj = jnp.dot(wide, weight_flat, preferred_element_type=jnp.float32)
    proj = proj.reshape(block_rows, 2, heads_kv, head_size)
    keys = (normalize(proj[:, 0]) * key_gain[0]).astype(jnp.bfloat16)
    values = proj[:, 1].astype(jnp.bfloat16)
    key_value = jnp.stack([keys, values], axis=1).reshape(block_rows, 2, kv_cols)
    qrows = query.astype(jnp.float32).reshape(text_rows, heads_kv, groups, head_size)
    qn = (normalize(qrows) * query_gain[0] * head_size ** (-0.5)).astype(jnp.bfloat16)
    block = lax.all_gather(key_value, "blk", axis=0, tiled=True)
    frames = lax.all_gather(image_frame, "blk", axis=0, tiled=True)
    count = block.shape[0]
    keys_part = block[:, 0].reshape(count, heads_kv, head_size)
    values_part = block[:, 1].reshape(count, heads_kv, head_size)
    scores = jnp.einsum("tkgd,skd->kgts", qn, keys_part, preferred_element_type=jnp.float32)
    allowed = frames[None, :] <= text_frame[:, None]
    weights = jnp.where(allowed, jnp.exp(scores), jnp.float32(0.0))
    total = jnp.sum(weights, axis=-1)
    wb = weights.astype(jnp.bfloat16)
    summed = jnp.einsum("kgts,skd->kgtd", wb, values_part, preferred_element_type=jnp.float32)
    result = summed / total[..., None]
    return (
        result.transpose(2, 0, 1, 3)
        .reshape(text_rows, heads_kv * groups * head_size)
        .astype(jnp.bfloat16)
    )


def solution(mesh):
    return jax.shard_map(
        per_device,
        mesh=mesh,
        in_specs=(
            P(("section", "blk"), "tp"),
            P(("section", "blk")),
            P("blk", ("section", "tp")),
            P("blk"),
            P("section", None, None, "tp"),
            P("section", None),
            P("section", None),
        ),
        out_specs=P(("section", "blk"), "tp"),
        check_vma=False,
    )
```

profile of v0, /device:TPU:0, one launch (start us, length us, event | category | flops | bytes accessed | tf_op | source)
XLA Modules:
  0.0 122.1 jit_solution(2899087948636825844)
XLA Ops:
  6.5 0.0 all-gather.4.cloned.1.call-start
  6.5 0.7 all-gather.4.cloned.1.call-update
  7.3 0.0 all-gather.6.cloned.1.call-start
  7.3 16.7 %copy.35 = bf16[1024,8,2,512]{3,1,2,0:T(8,128)(2,1)} copy(bf16[1024,8,2,512]{3,2,1,0:T(2,128)(2,1)} %bitcast.52) | data formatting | bytes 33554432
  24.0 21.3 %copy.22 = bf16[1024,8192]{1,0:T(8,128)(2,1)} copy(bf16[1024,8192]{0,1:T(8,128)(2,1)} %bitcast.49) | data formatting | bytes 33554432 | tf_op jit(solution)/shard_map/dot_general | solution.py:21
  45.3 3.4 %all-gather.4.cloned.1.call-done = bf16[256,8192]{1,0:T(8,128)(2,1)} async-done(((bf16[256,1024]{1,0:T(8,128)(2,1)}), bf16[256,8192]{1,0:T(8,128)(2,1)}) %all-gather.4.cloned.1.call-update) | async-done | bytes 4194320 | tf_op jit(solution)/shard_map/all_gather | solution.py:20
  48.7 0.0 copy-start.4
  48.7 0.0 copy-start
  48.7 9.4 %fusion.6 = f32[256,2,4,128]{0,3,2,1:T(8,128)S(1)} fusion(bf16[2,4,128,8192]{3,2,1,0:T(8,128)(2,1)} %bitcast.53, bf16[256,8192]{1,0:T(8,128)(2,1)} %all-gather.4.cloned.1.call-done), kind=kOutput, calls=%fused_computation.6 | convolution fusion | flops 4294967296 | bytes 22020096 | tf_op jit(solution)/shard_map/dot_general | solution.py:21
  58.2 0.1 multiply_reduce_fusion.1
  58.3 0.0 copy-done.4
  58.3 0.1 multiply_convert_fusion.1
  58.4 0.8 pad_maximum_fusion
  59.2 0.0 all-gather.6.cloned.1.call-update
  59.2 0.0 copy-done
  59.2 0.2 convert_bitcast_fusion
  59.5 0.0 copy-start.1
  59.5 0.0 copy-start.2
  59.5 0.0 copy-start.3
  59.5 0.4 copy.36
  59.9 0.8 multiply_reduce_fusion
  60.7 0.1 copy.23
  60.8 0.2 copy.24
  61.0 0.0 copy-done.1
  61.0 11.0 %all-gather = s32[4,1,256]{2,1,0:T(1,128)S(1)} all-gather(s32[1,1,256]{2,1,0:T(1,128)S(1)} %bitcast.61), channel_id=1, replica_groups=mesh['section'=4,'blk'=4,'tp'=2] {'blk'}, dimensions={0}, use_global_device_ids=true | all-gather | bytes 5120 | tf_op jit(solution)/shard_map/all_gather | solution.py:29
  72.0 0.0 copy-done.2
  72.0 0.2 broadcast_compare_fusion
  72.2 0.0 copy-done.3
  72.2 0.7 multiply_convert_fusion
  73.0 32.7 %all-gather.6.cloned.1.call-done = bf16[1024,2,512]{0,2,1:T(8,128)(2,1)} async-done(((bf16[256,2,512]{0,2,1:T(8,128)(2,1)}), bf16[1024,2,512]{0,2,1:T(8,128)(2,1)}) %all-gather.6.cloned.1.call-update) | async-done | bytes 2097168 | tf_op jit(solution)/shard_map/all_gather | solution.py:28
  105.6 1.7 %fusion.14 = (bf16[1024,1,512]{0,2,1:T(8,128)(2,1)S(1)}, bf16[1024,1,512]{0,2,1:T(8,128)(2,1)S(1)}) fusion(bf16[1024,2,512]{0,2,1:T(8,128)(2,1)} %all-gather.6.cloned.1.call-done), kind=kLoop, calls=%fused_computation.23 | loop fusion | bytes 4194304 | tf_op jit(solution)/shard_map/slice | solution.py:31
  107.4 3.4 %fusion = (f32[4,8,128]{2,1,0:T(8,128)S(1)}, f32[4,1024,128,8]{2,1,3,0:T(8,128)S(1)}) fusion(pred[128,1024]{0,1:T(8,128)(4,1)S(1)} %broadcast_compare_fusion, bf16[1024,4,128,1]{0,2,3,1:T(8,128)(2,1)S(1)} %bitcast.54, bf16[128,4,8,128]{3,2,1,0:T(8,128)(2,1)S(1)} %multiply_convert_fusion), kind=kOutput, calls=%fused_computation.1 | convolution fusion | flops 1082126336 | bytes 19021824 | tf_op jit(solution)/shard_map/tkgd,skd->kgts/dot_general | solution.py:33
  110.8 3.2 %fusion.8 = bf16[128,4,8,128]{0,3,2,1:T(8,128)(2,1)S(1)} fusion(bf16[1024,4,128,1]{0,2,3,1:T(8,128)(2,1)S(1)} %bitcast.57, f32[4,1024,128,8]{2,1,3,0:T(8,128)S(1)} %get-tuple-element.8, pred[128,1024]{0,1:T(8,128)(4,1)S(1)} %broadcast_compare_fusion, f32[128,4,8]{0,2,1:T(8,128)S(1)} %bitcast.60), kind=kOutput, calls=%fused_computation.9 | convolution fusion | flops 1083179008 | bytes 19021824 | tf_op jit(solution)/shard_map/kgts,skd->kgtd/dot_general | solution.py:38
  114.0 1.3 %copy.28 = bf16[128,4096]{1,0:T(8,128)(2,1)} copy(bf16[128,4096]{0,1:T(8,128)(2,1)S(1)} %bitcast.55) | data formatting | bytes 2097152 | tf_op jit(solution)/shard_map/convert_element_type | solution.py:43
  (3 shorter events, 0.0 us)
Async XLA Ops:
  6.5 42.2 %all-gather.4.cloned.1.call-start = ((), (), s32[]{:S(2)}) async-start(), calls=%async_computation | async-start | bytes 4718592 | tf_op jit(solution)/shard_map/all_gather | solution.py:20
  7.3 98.4 %all-gather.6.cloned.1.call-start = ((), (), s32[]{:S(2)}) async-start(), calls=%async_computation.1 | async-start | bytes 2621440 | tf_op jit(solution)/shard_map/all_gather | solution.py:28
  48.7 9.6 %copy-start.4 = (f32[1,128]{1,0:T(1,128)S(1)}, f32[1,128]{1,0:T(1,128)}, u32[]{:S(2)}) copy-start(f32[1,128]{1,0:T(1,128)} %param.13) | copy-start | bytes 1540
  48.7 10.5 %copy-start = (bf16[128,4096]{1,0:T(8,128)(2,1)S(1)}, bf16[128,4096]{1,0:T(8,128)(2,1)}, u32[]{:S(2)}) copy-start(bf16[128,4096]{1,0:T(8,128)(2,1)} %param.7) | copy-start | bytes 3145732
  59.5 1.5 %copy-start.1 = (s32[256]{0:T(256)S(1)}, s32[256]{0:T(256)}, u32[]{:S(2)}) copy-start(s32[256]{0:T(256)} %param.10) | copy-start | bytes 3076
  59.5 12.5 %copy-start.2 = (s32[128]{0:T(128)S(1)}, s32[128]{0:T(128)}, u32[]{:S(2)}) copy-start(s32[128]{0:T(128)} %param.8) | copy-start | bytes 1540
  59.5 12.7 %copy-start.3 = (f32[1,128]{1,0:T(1,128)S(1)}, f32[1,128]{1,0:T(1,128)}, u32[]{:S(2)}) copy-start(f32[1,128]{1,0:T(1,128)} %param.12) | copy-start | bytes 1540
Sparse Core Ops, SparseCore 0:
  9.3 39.4 all-gather.3
  59.4 46.2 all-gather.5
where the time goes:
time: 123 us; the launch traced here: 122 us
  local copies, waits for them, and re-layouts  41.7 us (34%)
  waiting for transfers between devices  36.8 us (30%)
  matrix products  16 us (13%)
  between operations  13.6 us (11%)
  blocking collectives  11 us (9%)
  other arithmetic  2.98 us (2%)
    all_gather x1, waiting for transfers between devices, per_device(): block = lax.all_gather(key_value, 'blk', axis=0, tiled=True)  32.7 us
    dot_general x1, local copies, waits for them, and re-layouts, per_device(): proj = jnp.dot(wide, weight_flat, preferred_element_type=jnp.float32)  21.3 us
    unnamed x12, local copies, waits for them, and re-layouts  17.1 us
    all_gather x1, blocking collectives, per_device(): frames = lax.all_gather(image_frame, 'blk', axis=0, tiled=True)  11 us
    dot_general x1, matrix products, per_device(): proj = jnp.dot(wide, weight_flat, preferred_element_type=jnp.float32)  9.44 us
    dot_general x1, matrix products, per_device(): jnp.einsum('tkgd,skd->kgts', qn, keys_part, preferred_element_type=jnp.fl...  3.4 us
    all_gather x1, waiting for transfers between devices, per_device(): wide = lax.all_gather(image_feats, ('section', 'tp'), axis=1, tiled=True)  3.39 us
    dot_general x1, matrix products, per_device(): jnp.einsum('kgts,skd->kgtd', wb, values_part, preferred_element_type=jnp....  3.22 us
  transfers between devices with their start and end apart: 2, of which 2 were waited for; matrix products, arithmetic and copies ran while one was open for 33% of the time, Pallas kernels for 0%

commit v1 on v0

--- a/solution.py
+++ b/solution.py
@@ -10,18 +10,16 @@
 
 def per_device(query, text_frame, image_feats, image_frame, kv_weight, query_gain, key_gain):
     head_size = query_gain.shape[1]
-    feat_width = kv_weight.shape[1]
     kv_cols = kv_weight.shape[3]
     heads_kv = kv_cols // head_size
     text_rows = query.shape[0]
     groups = query.shape[1] // kv_cols
     block_rows = image_feats.shape[0]
-    weight_flat = kv_weight[0].reshape(feat_width, 2 * kv_cols)
     wide = lax.all_gather(image_feats, ("section", "tp"), axis=1, tiled=True)
-    proj = jnp.dot(wide, weight_flat, preferred_element_type=jnp.float32)
-    proj = proj.reshape(block_rows, 2, heads_kv, head_size)
-    keys = (normalize(proj[:, 0]) * key_gain[0]).astype(jnp.bfloat16)
-    values = proj[:, 1].astype(jnp.bfloat16)
+    proj = jnp.einsum("rf,fkc->krc", wide, kv_weight[0], preferred_element_type=jnp.float32)
+    proj = proj.reshape(2, block_rows, heads_kv, head_size)
+    keys = (normalize(proj[0]) * key_gain[0]).astype(jnp.bfloat16)
+    values = proj[1].astype(jnp.bfloat16)
     key_value = jnp.stack([keys, values], axis=1).reshape(block_rows, 2, kv_cols)
     qrows = query.astype(jnp.float32).reshape(text_rows, heads_kv, groups, head_size)
     qn = (normalize(qrows) * query_gain[0] * head_size ** (-0.5)).astype(jnp.bfloat16)

time: 123 us -> 124 us (level)
  waiting for transfers between devices: 36.8 us -> 74.8 us
  local copies, waits for them, and re-layouts: 41.7 us -> 3.73 us
  matrix products: 16 us -> 17.9 us
    all_gather x1, waiting for transfers between devices: 3.39 us -> 41.4 us  [per_device(): wide = lax.all_gather(image_feats, ('section', 'tp'), axis=1, tiled=True)]
    dot_general x1 -> x0, local copies, waits for them, and re-layouts: 21.3 us -> none  [per_device(): proj = jnp.dot(wide, weight_flat, preferred_element_type=jnp.float32)]
    unnamed x12 -> x11, local copies, waits for them, and re-layouts: 17.1 us -> 0.4 us
    dot_general x1, matrix products: 9.44 us -> 11.1 us  [per_device(): jnp.einsum('rf,fkc->krc', wide, kv_weight[0], preferred_element_type=jnp....]
  transfers between devices with their start and end apart: 2 -> 2, of which waited for: 2 -> 2; matrix products, arithmetic and copies ran while one was open for 33% -> 2% of each run, Pallas kernels for 0% -> 0%
where the time goes in v1:
time: 124 us
  waiting for transfers between devices  74.8 us (60%)
  matrix products  17.9 us (14%)
  between operations  13.6 us (11%)
  blocking collectives  11 us (9%)
  local copies, waits for them, and re-layouts  3.73 us (3%)
  other arithmetic  3.09 us (2%)
    all_gather x1, waiting for transfers between devices, per_device(): wide = lax.all_gather(image_feats, ('section', 'tp'), axis=1, tiled=True)  41.4 us
    all_gather x1, waiting for transfers between devices, per_device(): block = lax.all_gather(key_value, 'blk', axis=0, tiled=True)  32.7 us
    dot_general x1, matrix products, per_device(): jnp.einsum('rf,fkc->krc', wide, kv_weight[0], preferred_element_type=jnp....  11.1 us
    all_gather x1, blocking collectives, per_device(): frames = lax.all_gather(image_frame, 'blk', axis=0, tiled=True)  11 us
    dot_general x1, matrix products, per_device(): jnp.einsum('tkgd,skd->kgts', qn, keys_part, preferred_element_type=jnp.fl...  3.47 us
    dot_general x1, matrix products, per_device(): jnp.einsum('kgts,skd->kgtd', wb, values_part, preferred_element_type=jnp....  3.28 us
  transfers between devices with their start and end apart: 2, of which 2 were waited for; matrix products, arithmetic and copies ran while one was open for 2% of the time, Pallas kernels for 0%

profile of v1, /device:TPU:0, one launch (start us, length us, event | category | flops | bytes accessed | tf_op | source)
XLA Modules:
  0.0 124.1 jit_solution(16487633910347299886)
XLA Ops:
  6.5 0.0 copy-start
  6.5 0.0 all-gather.4.cloned.1.call-start
  6.5 0.7 all-gather.4.cloned.1.call-update
  7.3 0.0 all-gather.6.cloned.1.call-start
  7.3 0.0 copy-done
  7.3 41.4 %all-gather.4.cloned.1.call-done = bf16[256,8192]{1,0:T(8,128)(2,1)} async-done(((bf16[256,1024]{1,0:T(8,128)(2,1)}), bf16[256,8192]{1,0:T(8,128)(2,1)}) %all-gather.4.cloned.1.call-update) | async-done | bytes 4194320 | tf_op jit(solution)/shard_map/all_gather | solution.py:18
  48.7 11.1 %fusion.12 = f32[2,256,512]{1,2,0:T(8,128)S(1)} fusion(bf16[256,8192]{1,0:T(8,128)(2,1)} %all-gather.4.cloned.1.call-done, bf16[8192,2,512]{2,1,0:T(2,128)(2,1)} %bitcast.69), kind=kOutput, calls=%fused_computation.14 | convolution fusion | flops 4294967296 | bytes 22020096 | tf_op jit(solution)/shard_map/rf,fkc->krc/dot_general | solution.py:19
  59.9 0.0 copy-start.1
  60.1 0.2 fusion.20
  60.2 0.8 pad_maximum_fusion
  61.1 0.0 all-gather.6.cloned.1.call-update
  61.1 0.0 copy-done.1
  61.1 0.2 convert_bitcast_fusion
  61.3 0.0 copy-start.2
  61.3 0.0 copy-start.3
  61.3 0.0 copy-start.4
  61.4 0.4 copy.30
  61.7 0.8 multiply_reduce_fusion
  62.6 0.1 copy.19
  62.7 0.2 copy.20
  62.8 0.0 copy-done.2
  62.8 11.0 %all-gather = s32[4,1,256]{2,1,0:T(1,128)S(1)} all-gather(s32[1,1,256]{2,1,0:T(1,128)S(1)} %bitcast.67), channel_id=1, replica_groups=mesh['section'=4,'blk'=4,'tp'=2] {'blk'}, dimensions={0}, use_global_device_ids=true | all-gather | bytes 5120 | tf_op jit(solution)/shard_map/all_gather | solution.py:27
  73.9 0.0 copy-done.3
  73.9 0.2 broadcast_compare_fusion
  74.1 0.0 copy-done.4
  74.1 0.7 multiply_convert_fusion
  74.8 32.7 %all-gather.6.cloned.1.call-done = bf16[1024,2,512]{0,2,1:T(8,128)(2,1)} async-done(((bf16[256,2,512]{0,2,1:T(8,128)(2,1)}), bf16[1024,2,512]{0,2,1:T(8,128)(2,1)}) %all-gather.6.cloned.1.call-update) | async-done | bytes 2097168 | tf_op jit(solution)/shard_map/all_gather | solution.py:26
  107.5 1.7 %fusion.23 = (bf16[1024,1,512]{0,2,1:T(8,128)(2,1)S(1)}, bf16[1024,1,512]{0,2,1:T(8,128)(2,1)S(1)}) fusion(bf16[1024,2,512]{0,2,1:T(8,128)(2,1)} %all-gather.6.cloned.1.call-done), kind=kLoop, calls=%fused_computation.29 | loop fusion | bytes 4194304 | tf_op jit(solution)/shard_map/slice | solution.py:29
  109.2 3.5 %fusion.2 = (f32[4,8,128]{2,1,0:T(8,128)S(1)}, f32[4,1024,128,8]{2,1,3,0:T(8,128)S(1)}) fusion(pred[128,1024]{0,1:T(8,128)(4,1)S(1)} %broadcast_compare_fusion, bf16[1024,4,128,1]{0,2,3,1:T(8,128)(2,1)S(1)} %bitcast.60, bf16[128,4,8,128]{3,2,1,0:T(8,128)(2,1)S(1)} %multiply_convert_fusion), kind=kOutput, calls=%fused_computation.3 | convolution fusion | flops 1082126336 | bytes 19021824 | tf_op jit(solution)/shard_map/tkgd,skd->kgts/dot_general | solution.py:31
  112.7 3.3 %fusion.9 = bf16[128,4,8,128]{0,3,2,1:T(8,128)(2,1)S(1)} fusion(bf16[1024,4,128,1]{0,2,3,1:T(8,128)(2,1)S(1)} %bitcast.64, f32[4,1024,128,8]{2,1,3,0:T(8,128)S(1)} %get-tuple-element.8, pred[128,1024]{0,1:T(8,128)(4,1)S(1)} %broadcast_compare_fusion, f32[128,4,8]{0,2,1:T(8,128)S(1)} %bitcast.66), kind=kOutput, calls=%fused_computation.10 | convolution fusion | flops 1083179008 | bytes 19021824 | tf_op jit(solution)/shard_map/kgts,skd->kgtd/dot_general | solution.py:36
  116.0 1.3 %copy.24 = bf16[128,4096]{1,0:T(8,128)(2,1)} copy(bf16[128,4096]{0,1:T(8,128)(2,1)S(1)} %bitcast.63) | data formatting | bytes 2097152 | tf_op jit(solution)/shard_map/convert_element_type | solution.py:41
  (7 shorter events, 0.2 us)
Async XLA Ops:
  6.5 0.8 copy-start
  6.5 42.2 %all-gather.4.cloned.1.call-start = ((), (), s32[]{:S(2)}) async-start(), calls=%async_computation | async-start | bytes 4718592 | tf_op jit(solution)/shard_map/all_gather | solution.py:18
  7.3 100.3 %all-gather.6.cloned.1.call-start = ((), (), s32[]{:S(2)}) async-start(), calls=%async_computation.1 | async-start | bytes 2621440 | tf_op jit(solution)/shard_map/all_gather | solution.py:26
  59.9 1.2 %copy-start.1 = (bf16[128,4096]{1,0:T(8,128)(2,1)S(1)}, bf16[128,4096]{1,0:T(8,128)(2,1)}, u32[]{:S(2)}) copy-start(bf16[128,4096]{1,0:T(8,128)(2,1)} %param.7) | copy-start | bytes 3145732
  61.3 1.5 %copy-start.2 = (s32[256]{0:T(256)S(1)}, s32[256]{0:T(256)}, u32[]{:S(2)}) copy-start(s32[256]{0:T(256)} %param.10) | copy-start | bytes 3076
  61.3 12.5 %copy-start.3 = (s32[128]{0:T(128)S(1)}, s32[128]{0:T(128)}, u32[]{:S(2)}) copy-start(s32[128]{0:T(128)} %param.8) | copy-start | bytes 1540
  61.3 12.7 %copy-start.4 = (f32[1,128]{1,0:T(1,128)S(1)}, f32[1,128]{1,0:T(1,128)}, u32[]{:S(2)}) copy-start(f32[1,128]{1,0:T(1,128)} %param.12) | copy-start | bytes 1540
Sparse Core Ops, SparseCore 0:
  9.3 39.4 all-gather.3
  61.2 46.2 all-gather.5

commit v2 on v1

v2 whole, which is shorter than its diff:
```python
import functools

import jax
import jax.numpy as jnp
from jax import lax
from jax.experimental import pallas as pl
from jax.experimental.pallas import tpu as pltpu
from jax.sharding import PartitionSpec as P

MESH = pl.DeviceIdType.MESH
BF16 = jnp.bfloat16
F32 = jnp.float32
EPS = 1e-05


def kernel(
    dims,
    q_ref, tf_ref, x_ref, fr_ref, w_ref, qg_ref, kg_ref,
    out_ref,
    stage, kvw, xg, kv, frames, qn, acc, tot, proj,
    wsem, fsend, frecv, ssend, srecv, rsend, rrecv, zsend, zrecv,
):
    n_sec, n_blk, n_tp, n_chunk, w_rows = dims
    sec, blk, tp = lax.axis_index("section"), lax.axis_index("blk"), lax.axis_index("tp")
    par = lax.rem(sec, 2)
    half = sec // 2
    mine = half * n_tp + tp
    n_half = n_sec // 2
    n_group = n_half * n_tp
    rows, fw = x_ref.shape
    rc = rows // n_chunk
    feats, _, kv_cols = w_ref.shape[1:]
    head = qg_ref.shape[1]
    heads_kv = kv_cols // head
    text = q_ref.shape[0]
    groups = q_ref.shape[1] // kv_cols
    n_w = feats // w_rows
    n_stage = stage.shape[0]
    sibling = {"section": sec + 1 - 2 * par}

    def w_copy(i):
        return pltpu.make_async_copy(
            w_ref.at[0, pl.ds(i * w_rows, w_rows)], stage.at[i % n_stage], wsem.at[i % n_stage]
        )

    for i in range(min(n_stage, n_w)):
        w_copy(i).start()

    def plane_peer(k):
        other = lax.rem(mine + k, n_group)
        return {"section": 2 * (other // n_tp) + par, "tp": lax.rem(other, n_tp)}

    def line_peer(k):
        return {"blk": lax.rem(blk + k, n_blk)}

    barrier = pltpu.get_barrier_semaphore()
    pl.semaphore_signal(barrier, inc=1, device_id=sibling, device_id_type=MESH)
    for k in range(1, n_group):
        pl.semaphore_signal(barrier, inc=1, device_id=plane_peer(k), device_id_type=MESH)
    for k in range(1, n_blk):
        pl.semaphore_signal(barrier, inc=1, device_id=line_peer(k), device_id_type=MESH)
    pl.semaphore_wait(barrier, n_group + n_blk - 1)

    def feature_copy(c, k):
        return pltpu.make_async_remote_copy(
            src_ref=x_ref.at[pl.ds(c * rc, rc)],
            dst_ref=xg.at[c, par, mine],
            send_sem=fsend.at[c],
            recv_sem=frecv.at[c],
            device_id=plane_peer(k),
            device_id_type=MESH,
        )

    for c in range(n_chunk):
        pltpu.make_async_copy(x_ref.at[pl.ds(c * rc, rc)], xg.at[c, par, mine], frecv.at[c]).start()
        for k in range(1, n_group):
            feature_copy(c, k).start()

    def frame_copy(k):
        return pltpu.make_async_remote_copy(
            src_ref=fr_ref,
            dst_ref=frames.at[blk],
            send_sem=rsend,
            recv_sem=rrecv,
            device_id=line_peer(k),
            device_id_type=MESH,
        )

    pltpu.make_async_copy(fr_ref, frames.at[blk], rrecv).start()
    for k in range(1, n_blk):
        frame_copy(k).start()

    def share(c):
        return pltpu.make_async_remote_copy(
            src_ref=xg.at[c, par],
            dst_ref=xg.at[c, par],
            send_sem=ssend.at[c],
            recv_sem=srecv.at[c],
            device_id=sibling,
            device_id_type=MESH,
        )

    def pass_on(c):
        pltpu.make_async_copy(xg.at[c, par], xg.at[c, par], frecv.at[c]).wait()
        share(c).start()

    gain = qg_ref[...] * head ** (-0.5)

    @pl.loop(0, heads_kv)
    def _(k):
        for g in range(groups):
            col = pl.multiple_of((k * groups + g) * head, head)
            rowsq = q_ref[:, pl.ds(col, head)].astype(F32)
            scale = lax.rsqrt(jnp.mean(rowsq * rowsq, axis=-1, keepdims=True) + EPS)
            qn[k, g * text:(g + 1) * text, :] = (rowsq * scale * gain).astype(BF16)

    sub = 2 * head
    ri = lax.broadcasted_iota(jnp.int32, (sub, sub), 0)
    ci = lax.broadcasted_iota(jnp.int32, (sub, sub), 1)
    take = (ci == 2 * lax.rem(ri, head) + ri // head).astype(BF16)
    for i in range(n_w):
        w_copy(i).wait()

        @pl.loop(0, w_rows // head)
        def _(j):
            at = pl.multiple_of(j * head, head)
            block = stage[i % n_stage, pl.ds(at, head)].reshape(sub, kv_cols)
            apart = jnp.dot(take, block, preferred_element_type=F32).astype(BF16)
            to = pl.multiple_of(i * w_rows + j * head, head)
            kvw[pl.ds(to, head), :kv_cols] = apart[:head]
            kvw[pl.ds(to, head), kv_cols:] = apart[head:]

        if i + n_stage < n_w:
            w_copy(i + n_stage).start()
        if i == n_w // 2:
            pass_on(0)

    def line_copy(way, src, d, c):
        to = blk + 1 if way == 0 else blk - 1
        return pltpu.make_async_remote_copy(
            src_ref=kv.at[src, c],
            dst_ref=kv.at[src, c],
            send_sem=zsend.at[way, d - 1, c],
            recv_sem=zrecv.at[way, d - 1, c],
            device_id={"blk": to},
            device_id_type=MESH,
        )

    can = (blk + 1 < n_blk, blk >= 1)

    def source(way, d):
        return blk - d if way == 0 else blk + d

    def exists(way, d):
        return blk - d >= 0 if way == 0 else blk + d < n_blk

    def relay(way, d, c):
        @pl.when(exists(way, d))
        def _():
            src = source(way, d)
            line_copy(way, src, d, c).wait_recv()

            @pl.when(can[way])
            def _():
                line_copy(way, src, d + 1, c).start()

    for c in range(n_chunk):
        if c + 1 < n_chunk:
            pass_on(c + 1)
        share(c).wait_recv()
        proj[...] = jnp.zeros_like(proj)

        @pl.loop(0, n_group)
        def _(j):
            for p in range(2):
                place = ((2 * (j // n_tp) + p) * n_tp + lax.rem(j, n_tp)) * fw
                part = kvw[pl.ds(pl.multiple_of(place, fw), fw), :]
                proj[...] += jnp.dot(xg[c, p, j], part, preferred_element_type=F32)

        for h in range(heads_kv):
            key = proj[:, h * head:(h + 1) * head]
            scale = lax.rsqrt(jnp.mean(key * key, axis=-1, keepdims=True) + EPS)
            kv[blk, c, :, h * head:(h + 1) * head] = (key * scale * kg_ref[...]).astype(BF16)
        kv[blk, c, :, kv_cols:] = proj[:, kv_cols:].astype(BF16)
        for way in range(2):
            @pl.when(can[way])
            def _():
                line_copy(way, blk, 1, c).start()
        if c >= 1:
            for way in range(2):
                relay(way, 1, c - 1)

    pltpu.make_async_copy(frames, frames, rrecv).wait()
    limit = jnp.broadcast_to(tf_ref[...], (text, text)).T[:, :1]
    acc[...] = jnp.zeros_like(acc)
    tot[...] = jnp.zeros_like(tot)

    def attend(src):
        allowed = frames[src] <= limit

        @pl.loop(0, heads_kv)
        def _(k):
            at = pl.multiple_of(k * head, head)
            keys = kv[src, :, :, pl.ds(at, head)].reshape(rows, head)
            values = kv[src, :, :, pl.ds(kv_cols + at, head)].reshape(rows, head)
            for g in range(groups):
                span = slice(g * text, (g + 1) * text)
                scores = lax.dot_general(
                    qn[k, span, :], keys, (((1,), (1,)), ((), ())), preferred_element_type=F32
                )
                weights = jnp.where(allowed, jnp.exp(scores), 0.0)
                total = weights[:, :head]
                for m in range(1, rows // head):
                    total = total + weights[:, m * head:(m + 1) * head]
                tot[k, span, :] += total
                acc[k, span, :] += jnp.dot(
                    weights.astype(BF16), values, preferred_element_type=F32
                )

    def attend_if(way, d):
        @pl.when(exists(way, d))
        def _():
            attend(source(way, d))

    for way in range(2):
        relay(way, 1, n_chunk - 1)
    attend(blk)

    @pl.loop(1, n_blk - 1)
    def _(d):
        for c in range(n_chunk):
            for way in range(2):
                relay(way, d + 1, c)
        for way in range(2):
            attend_if(way, d)

    for way in range(2):
        attend_if(way, n_blk - 1)

    @pl.loop(0, heads_kv)
    def _(k):
        for g in range(groups):
            span = slice(g * text, (g + 1) * text)
            total = jnp.sum(tot[k, span, :], axis=-1, keepdims=True)
            col = pl.multiple_of((k * groups + g) * head, head)
            out_ref[:, pl.ds(col, head)] = (acc[k, span, :] / total).astype(BF16)

    for c in range(n_chunk):
        if n_group > 1:
            gone = xg.at[c, par, pl.ds(0, n_group - 1)]
            pltpu.make_async_copy(gone, gone, fsend.at[c]).wait()
        share(c).wait_send()
    if n_blk > 1:
        gone = frames.at[pl.ds(0, n_blk - 1)]
        pltpu.make_async_copy(gone, gone, rsend).wait()

    @pl.loop(1, n_blk)
    def _(d):
        for way in range(2):
            @pl.when(can[way] & exists(way, d - 1))
            def _():
                for c in range(n_chunk):
                    line_copy(way, source(way, d - 1), d, c).wait_send()


def solution(mesh):
    n_sec, n_blk, n_tp = mesh.shape["section"], mesh.shape["blk"], mesh.shape["tp"]

    def per_device(query, text_frame, image_feats, image_frame, kv_weight, query_gain, key_gain):
        text = query.shape[0]
        rows, fw = image_feats.shape
        feats, _, kv_cols = kv_weight.shape[1:]
        head = query_gain.shape[1]
        heads_kv = kv_cols // head
        groups = query.shape[1] // kv_cols
        n_chunk = 4
        rc = rows // n_chunk
        w_rows = 1024
        n_stage = 4
        n_group = n_sec // 2 * n_tp
        vmem = pl.BlockSpec(memory_space=pltpu.VMEM)
        dma = pltpu.SemaphoreType.DMA
        return pl.pallas_call(
            functools.partial(kernel, (n_sec, n_blk, n_tp, n_chunk, w_rows)),
            out_shape=jax.ShapeDtypeStruct(query.shape, BF16),
            in_specs=[vmem, vmem, vmem, vmem, pl.BlockSpec(memory_space=pl.ANY), vmem, vmem],
            out_specs=vmem,
            scratch_shapes=[
                pltpu.VMEM((n_stage, w_rows, 2, kv_cols), BF16),
                pltpu.VMEM((feats, 2 * kv_cols), BF16),
                pltpu.VMEM((n_chunk, 2, n_group, rc, fw), BF16),
                pltpu.VMEM((n_blk, n_chunk, rc, 2 * kv_cols), BF16),
                pltpu.VMEM((n_blk, 1, rows), jnp.int32),
                pltpu.VMEM((heads_kv, groups * text, head), BF16),
                pltpu.VMEM((heads_kv, groups * text, head), F32),
                pltpu.VMEM((heads_kv, groups * text, head), F32),
                pltpu.VMEM((rc, 2 * kv_cols), F32),
                dma((n_stage,)),
                dma((n_chunk,)),
                dma((n_chunk,)),
                dma((n_chunk,)),
                dma((n_chunk,)),
                dma,
                dma,
                dma((2, n_blk, n_chunk)),
                dma((2, n_blk, n_chunk)),
            ],
            compiler_params=pltpu.CompilerParams(
                collective_id=0, has_side_effects=True, vmem_limit_bytes=56 << 20
            ),
        )(
            query,
            text_frame.reshape(1, text),
            image_feats,
            image_frame.reshape(1, rows),
            kv_weight,
            query_gain,
            key_gain,
        )

    return jax.shard_map(
        per_device,
        mesh=mesh,
        in_specs=(
            P(("section", "blk"), "tp"),
            P(("section", "blk")),
            P("blk", ("section", "tp")),
            P("blk"),
            P("section", None, None, "tp"),
            P("section", None),
            P("section", None),
        ),
        out_specs=P(("section", "blk"), "tp"),
        check_vma=False,
    )
```

time: 124 us -> 72.6 us (0.59)
  waiting for transfers between devices: 74.8 us -> 0 us
  Pallas kernels: 0 us -> 70.2 us
  matrix products: 17.9 us -> 0 us
  between operations: 13.6 us -> 0.01 us
  blocking collectives: 11 us -> 0 us
  other arithmetic: 3.09 us -> 0 us
  local copies, waits for them, and re-layouts: 3.73 us -> 2.29 us
    all_gather x2 -> x0, waiting for transfers between devices: 74.1 us -> none  [the longest x1 41.4 us: per_device(): wide = lax.all_gather(image_feats, ('section', 'tp'), axis=1, tiled=True)]
    pallas_call x0 -> x1, Pallas kernels: none -> 70.2 us  [per_device(): pl.pallas_call(functools.partial(kernel, (n_sec, n_blk, n_tp, n_chunk, w_...]
    dot_general x3 -> x0, matrix products: 17.9 us -> none  [the longest x1 11.1 us: per_device(): jnp.einsum('rf,fkc->krc', wide, kv_weight[0], preferred_element_type=jnp....]
    all_gather x1 -> x0, blocking collectives: 11 us -> none  [per_device(): frames = lax.all_gather(image_frame, 'blk', axis=0, tiled=True)]
    unnamed x11 -> x1, local copies, waits for them, and re-layouts: 0.4 us -> 2.29 us
    slice x1 -> x0, local copies, waits for them, and re-layouts: 1.71 us -> none  [per_device(): keys_part = block[:, 0].reshape(count, heads_kv, head_size)]
    convert_element_type x2 -> x0, local copies, waits for them, and re-layouts: 1.34 us -> none  [the longest x1 1.31 us: per_device(): return result.transpose(2, 0, 1, 3).reshape(text_rows, heads_kv * groups...]
  transfers between devices with their start and end apart: 2 -> 0, of which waited for: 2 -> 0; matrix products, arithmetic and copies ran while one was open for 2% -> 0% of each run, Pallas kernels for 0% -> 0%
where the time goes in v2:
time: 72.6 us; the launch traced here: 72.4 us
  Pallas kernels  70.2 us (97%)
  local copies, waits for them, and re-layouts  2.29 us (3%)
    pallas_call x1, Pallas kernels, per_device(): pl.pallas_call(functools.partial(kernel, (n_sec, n_blk, n_tp, n_chunk, w_...  70.2 us
    unnamed x1, local copies, waits for them, and re-layouts  2.29 us

profile of v2, /device:TPU:0, one launch (start us, length us, event | category | flops | bytes accessed | tf_op | source)
XLA Modules:
  0.0 72.4 jit_solution(8168574517388361318)
XLA Ops:
  0.0 70.2 %shard_map.73 = bf16[128,4096]{1,0:T(8,128)(2,1)} custom-call(bf16[128,4096]{1,0:T(8,128)(2,1)} %q_ref.1, s32[1,128]{1,0:T(1,128)} %bitcast.3, bf16[256,1024]{1,0:T(8,128)(2,1)} %x_ref.1, s32[1,256]{1,0:T(1,128)} %bitcast.2, bf16[1,8192,2,512]{3,2,1,0:T(2,128)(2,1)} %w_ref.1, f32[1,128]{1,0:T(1,128)} %qg_ref.1, f32[1,128]{1,0:T(1,128)} %kg_ref.1), custom_call_target="tpu_custom_call" | custom-call | tf_op jit(solution)/shard_map/pallas_call | solution.py:283
  70.2 2.3 %copy.9 = bf16[128,4096]{1,0:T(8,128)(2,1)} copy(bf16[128,4096]{1,0:T(8,128)(2,1)} %shard_map.73) | data formatting | bytes 2097152

commit v3 on v2

--- a/solution.py
+++ b/solution.py
@@ -61,20 +61,60 @@
         pl.semaphore_signal(barrier, inc=1, device_id=line_peer(k), device_id_type=MESH)
     pl.semaphore_wait(barrier, n_group + n_blk - 1)
 
+    square = n_half == 2 and n_tp == 2
+    near = ({"section": 2 * (1 - half) + par}, {"tp": 1 - tp})
+    near_at = ((1 - half) * n_tp + tp, half * n_tp + 1 - tp)
+
     def feature_copy(c, k):
         return pltpu.make_async_remote_copy(
             src_ref=x_ref.at[pl.ds(c * rc, rc)],
             dst_ref=xg.at[c, par, mine],
-            send_sem=fsend.at[c],
-            recv_sem=frecv.at[c],
-            device_id=plane_peer(k),
-            device_id_type=MESH,
-        )
-
-    for c in range(n_chunk):
-        pltpu.make_async_copy(x_ref.at[pl.ds(c * rc, rc)], xg.at[c, par, mine], frecv.at[c]).start()
-        for k in range(1, n_group):
+            send_sem=fsend.at[c, k if square else 0],
+            recv_sem=frecv.at[c, k if square else 2],
+            device_id=near[k] if square else plane_peer(k),
+            device_id_type=MESH,
+        )
+
+    def arrived(c, k):
+        return pltpu.make_async_remote_copy(
+            src_ref=x_ref.at[pl.ds(c * rc, rc)],
+            dst_ref=xg.at[c, par, near_at[k]],
+            send_sem=fsend.at[c, k],
+            recv_sem=frecv.at[c, k],
+            device_id=near[k],
+            device_id_type=MESH,
+        )
+
+    def corner_copy(c, k, at):
+        part = xg.at[c, par, at, pl.ds(k * (rc // 2), rc // 2)]
+        return pltpu.make_async_remote_copy(
+            src_ref=part,
+            dst_ref=part,
+            send_sem=fsend.at[c, 2 + k],
+            recv_sem=frecv.at[c, 3 + k],
+            device_id=near[1 - k],
+            device_id_type=MESH,
+        )
+
+    def local_copy(c):
+        return pltpu.make_async_copy(
+            x_ref.at[pl.ds(c * rc, rc)], xg.at[c, par, mine], frecv.at[c, 2]
+        )
+
+    def start(c):
+        for k in range(2) if square else range(1, n_group):
             feature_copy(c, k).start()
+        local_copy(c).start()
+
+    def forward(c):
+        if square:
+            for k in range(2):
+                arrived(c, k).wait_recv()
+                corner_copy(c, k, near_at[k]).start()
+
+    start(0)
+    if n_chunk > 1:
+        start(1)
 
     def frame_copy(k):
         return pltpu.make_async_remote_copy(
@@ -101,18 +141,13 @@
         )
 
     def pass_on(c):
-        pltpu.make_async_copy(xg.at[c, par], xg.at[c, par], frecv.at[c]).wait()
+        if square:
+            local_copy(c).wait()
+            for k in range(2):
+                corner_copy(c, k, (1 - half) * n_tp + 1 - tp).wait_recv()
+        else:
+            pltpu.make_async_copy(xg.at[c, par], xg.at[c, par], frecv.at[c, 2]).wait()
         share(c).start()
-
-    gain = qg_ref[...] * head ** (-0.5)
-
-    @pl.loop(0, heads_kv)
-    def _(k):
-        for g in range(groups):
-            col = pl.multiple_of((k * groups + g) * head, head)
-            rowsq = q_ref[:, pl.ds(col, head)].astype(F32)
-            scale = lax.rsqrt(jnp.mean(rowsq * rowsq, axis=-1, keepdims=True) + EPS)
-            qn[k, g * text:(g + 1) * text, :] = (rowsq * scale * gain).astype(BF16)
 
     sub = 2 * head
     ri = lax.broadcasted_iota(jnp.int32, (sub, sub), 0)
@@ -121,7 +156,7 @@
     for i in range(n_w):
         w_copy(i).wait()
 
-        @pl.loop(0, w_rows // head)
+        @pl.loop(0, w_rows // head, unroll=4)
         def _(j):
             at = pl.multiple_of(j * head, head)
             block = stage[i % n_stage, pl.ds(at, head)].reshape(sub, kv_cols)
@@ -132,8 +167,16 @@
 
         if i + n_stage < n_w:
             w_copy(i + n_stage).start()
-        if i == n_w // 2:
+        if i == n_w // 8:
+            forward(0)
+            if n_chunk > 2:
+                start(2)
+        if i == (3 * n_w) // 8:
             pass_on(0)
+        if i == (5 * n_w) // 8 and n_chunk > 1:
+            forward(1)
+            if n_chunk > 3:
+                start(3)
 
     def line_copy(way, src, d, c):
         to = blk + 1 if way == 0 else blk - 1
@@ -165,8 +208,6 @@
                 line_copy(way, src, d + 1, c).start()
 
     for c in range(n_chunk):
-        if c + 1 < n_chunk:
-            pass_on(c + 1)
         share(c).wait_recv()
         proj[...] = jnp.zeros_like(proj)
 
@@ -186,9 +227,25 @@
             @pl.when(can[way])
             def _():
                 line_copy(way, blk, 1, c).start()
+        if c + 1 < n_chunk:
+            pass_on(c + 1)
+        if c + 2 < n_chunk:
+            forward(c + 2)
+        if c + 4 < n_chunk:
+            start(c + 4)
         if c >= 1:
             for way in range(2):
                 relay(way, 1, c - 1)
+
+    gain = qg_ref[...] * head ** (-0.5)
+
+    @pl.loop(0, heads_kv)
+    def _(k):
+        for g in range(groups):
+            col = pl.multiple_of((k * groups + g) * head, head)
+            rowsq = q_ref[:, pl.ds(col, head)].astype(F32)
+            scale = lax.rsqrt(jnp.mean(rowsq * rowsq, axis=-1, keepdims=True) + EPS)
+            qn[k, g * text:(g + 1) * text, :] = (rowsq * scale * gain).astype(BF16)
 
     pltpu.make_async_copy(frames, frames, rrecv).wait()
     limit = jnp.broadcast_to(tf_ref[...], (text, text)).T[:, :1]
@@ -231,8 +288,8 @@
         for c in range(n_chunk):
             for way in range(2):
                 relay(way, d + 1, c)
-        for way in range(2):
-            attend_if(way, d)
+            if c < 2:
+                attend_if(c, d)
 
     for way in range(2):
         attend_if(way, n_blk - 1)
@@ -246,9 +303,13 @@
             out_ref[:, pl.ds(col, head)] = (acc[k, span, :] / total).astype(BF16)
 
     for c in range(n_chunk):
-        if n_group > 1:
+        if square:
+            for k in range(2):
+                feature_copy(c, k).wait_send()
+                corner_copy(c, k, near_at[k]).wait_send()
+        elif n_group > 1:
             gone = xg.at[c, par, pl.ds(0, n_group - 1)]
-            pltpu.make_async_copy(gone, gone, fsend.at[c]).wait()
+            pltpu.make_async_copy(gone, gone, fsend.at[c, 0]).wait()
         share(c).wait_send()
     if n_blk > 1:
         gone = frames.at[pl.ds(0, n_blk - 1)]
@@ -296,8 +357,8 @@
                 pltpu.VMEM((heads_kv, groups * text, head), F32),
                 pltpu.VMEM((rc, 2 * kv_cols), F32),
                 dma((n_stage,)),
-                dma((n_chunk,)),
-                dma((n_chunk,)),
+                dma((n_chunk, 4)),
+                dma((n_chunk, 5)),
                 dma((n_chunk,)),
                 dma((n_chunk,)),
                 dma,

time: 72.6 us -> 68.4 us (0.942)
  Pallas kernels: 70.2 us -> 66 us
    pallas_call x1, Pallas kernels: 70.2 us -> 66 us  [per_device(): pl.pallas_call(functools.partial(kernel, (n_sec, n_blk, n_tp, n_chunk, w_...]
where the time goes in v3:
time: 68.4 us; the launch traced here: 68.2 us
  Pallas kernels  66 us (96%)
  local copies, waits for them, and re-layouts  2.29 us (3%)
    pallas_call x1, Pallas kernels, per_device(): pl.pallas_call(functools.partial(kernel, (n_sec, n_blk, n_tp, n_chunk, w_...  66 us
    unnamed x1, local copies, waits for them, and re-layouts  2.29 us

profile of v3, /device:TPU:0, one launch (start us, length us, event | category | flops | bytes accessed | tf_op | source)
XLA Modules:
  0.0 68.2 jit_solution(17764507294440961291)
XLA Ops:
  0.0 66.0 %shard_map.73 = bf16[128,4096]{1,0:T(8,128)(2,1)} custom-call(bf16[128,4096]{1,0:T(8,128)(2,1)} %q_ref.1, s32[1,128]{1,0:T(1,128)} %bitcast.3, bf16[256,1024]{1,0:T(8,128)(2,1)} %x_ref.1, s32[1,256]{1,0:T(1,128)} %bitcast.2, bf16[1,8192,2,512]{3,2,1,0:T(2,128)(2,1)} %w_ref.1, f32[1,128]{1,0:T(1,128)} %qg_ref.1, f32[1,128]{1,0:T(1,128)} %kg_ref.1), custom_call_target="tpu_custom_call" | custom-call | tf_op jit(solution)/shard_map/pallas_call | solution.py:344
  66.0 2.3 %copy.9 = bf16[128,4096]{1,0:T(8,128)(2,1)} copy(bf16[128,4096]{1,0:T(8,128)(2,1)} %shard_map.73) | data formatting | bytes 2097152

commit v4 on v3

--- a/solution.py
+++ b/solution.py
@@ -211,7 +211,7 @@
         share(c).wait_recv()
         proj[...] = jnp.zeros_like(proj)
 
-        @pl.loop(0, n_group)
+        @pl.loop(0, n_group, unroll=2)
         def _(j):
             for p in range(2):
                 place = ((2 * (j // n_tp) + p) * n_tp + lax.rem(j, n_tp)) * fw
@@ -229,13 +229,13 @@
                 line_copy(way, blk, 1, c).start()
         if c + 1 < n_chunk:
             pass_on(c + 1)
+        if c >= 1:
+            for way in range(2):
+                relay(way, 1, c - 1)
         if c + 2 < n_chunk:
             forward(c + 2)
         if c + 4 < n_chunk:
             start(c + 4)
-        if c >= 1:
-            for way in range(2):
-                relay(way, 1, c - 1)
 
     gain = qg_ref[...] * head ** (-0.5)
 

time: 68.4 us -> 68.3 us (level)
  no operation moved by 1% of the time
where the time goes in v4:
time: 68.3 us; the launch traced here: 68.2 us
  Pallas kernels  65.9 us (96%)
  local copies, waits for them, and re-layouts  2.29 us (3%)
    pallas_call x1, Pallas kernels, per_device(): pl.pallas_call(functools.partial(kernel, (n_sec, n_blk, n_tp, n_chunk, w_...  65.9 us
    unnamed x1, local copies, waits for them, and re-layouts  2.29 us

profile of v4, /device:TPU:0, one launch (start us, length us, event | category | flops | bytes accessed | tf_op | source)
XLA Modules:
  0.0 68.2 jit_solution(16543501662780302615)
XLA Ops:
  0.0 65.9 %shard_map.73 = bf16[128,4096]{1,0:T(8,128)(2,1)} custom-call(bf16[128,4096]{1,0:T(8,128)(2,1)} %q_ref.1, s32[1,128]{1,0:T(1,128)} %bitcast.3, bf16[256,1024]{1,0:T(8,128)(2,1)} %x_ref.1, s32[1,256]{1,0:T(1,128)} %bitcast.2, bf16[1,8192,2,512]{3,2,1,0:T(2,128)(2,1)} %w_ref.1, f32[1,128]{1,0:T(1,128)} %qg_ref.1, f32[1,128]{1,0:T(1,128)} %kg_ref.1), custom_call_target="tpu_custom_call" | custom-call | tf_op jit(solution)/shard_map/pallas_call | solution.py:344
  65.9 2.3 %copy.9 = bf16[128,4096]{1,0:T(8,128)(2,1)} copy(bf16[128,4096]{1,0:T(8,128)(2,1)} %shard_map.73) | data formatting | bytes 2097152
